TPU v7x, 32 devices: a whole 2x2x4 slice. The times are simulated.
32 devices in a mesh: groups: 2 (over y), ctx: 4 (over z), head: 2 (over x), sub: 2 (over core).
Axes of the slice: x: 2, y: 2, z: 4, core: 2. Of those that a mesh axis runs over, the one named last changes fastest.
Arguments:
- queries: bfloat16 [3072, 8192], P(('groups', 'ctx'), ('head', 'sub')), parts along dimension 0, may hold values from -60 to 60
- key_rows: bfloat16 [3072, 1024], P(('groups', 'ctx'), 'head'), parts along dimension 0, may hold values from -6 to 6
- value_rows: bfloat16 [3072, 1024], P(('groups', 'ctx'), 'head'), parts along dimension 0, may hold values from -6 to 6
- out_weight: bfloat16 [8192, 5120], P(('head', 'sub'), 'ctx'), may hold values from -0.375 to 0.375
Outputs:
- mixed: bfloat16 [3072, 5120], P(('groups', 'ctx'), ('head', 'sub')), parts along dimension 0
There are 2 independent parts, one for each index of `groups`. A program takes and returns all parts, laid end to end along the dimension named above; an argument that names none is the same for every part. Nothing has to cross between parts.
All inputs are finite; a program needn't handle non-finite values.
Results may differ from a plain program's by a relative error of at most 0.02.
Values may be sent and summed in bfloat16 or wider, within the bound.
A program may use at most 128 MiB of HBM per device.

v0:
```python
import jax
import jax.numpy as jnp
from jax import lax
from jax.sharding import PartitionSpec as P

QH = 64
KVH = 8
HD = 128


def from_behind(block, axis, distance):
    devices = range(lax.axis_size(axis))
    route = [((i - distance) % len(devices), i) for i in devices]
    return lax.ppermute(block, axis, route)


def on_device(queries, key_rows, value_rows, out_weight):
    token_count = queries.shape[0]
    heads_here = queries.shape[1] // HD
    pairs_here = key_rows.shape[1] // HD
    group_ratio = QH // KVH
    pairs_read = max(heads_here // group_ratio, 1)
    per_pair = heads_here // pairs_read
    head_offset = lax.axis_index("sub") * heads_here // group_ratio
    keys_read = lax.dynamic_slice_in_dim(
        key_rows.reshape(token_count, pairs_here, HD), head_offset, pairs_read, 1
    )
    values_read = lax.dynamic_slice_in_dim(
        value_rows.reshape(token_count, pairs_here, HD), head_offset, pairs_read, 1
    )
    stacked = jnp.stack([keys_read, values_read])
    grouped = queries.reshape(token_count, pairs_read, per_pair, HD)
    factor = 1.0 / HD**0.5

    def absorb(running, key_block, value_block):
        old_max, old_sum, old_out = running
        scores = (
            jnp.einsum("tngd,knd->tngk", grouped, key_block, preferred_element_type=jnp.float32)
            * factor
        )
        new_max = jnp.maximum(old_max, jnp.max(scores, axis=-1))
        shrink = jnp.exp(old_max - new_max)
        expo = jnp.exp(scores - new_max[..., None])
        new_sum = old_sum * shrink + jnp.sum(expo, axis=-1)
        added = jnp.einsum(
            "tngk,knd->tngd",
            expo.astype(jnp.bfloat16),
            value_block,
            preferred_element_type=jnp.float32,
        )
        return (new_max, new_sum, old_out * shrink[..., None] + added)

    empty = (
        jnp.full((token_count, pairs_read, per_pair), -1e30, jnp.float32),
        jnp.zeros((token_count, pairs_read, per_pair), jnp.float32),
        jnp.zeros((token_count, pairs_read, per_pair, HD), jnp.float32),
    )
    cycle_size = lax.axis_size("ctx")

    def forward(blocks):
        return from_behind(blocks, "ctx", 1)

    def both_turn(turn_index, loop_state):
        ahead, behind, running = loop_state
        ahead = forward(ahead)
        behind = from_behind(behind, "ctx", -1)
        running = absorb(running, ahead[0], ahead[1])
        return (ahead, behind, absorb(running, behind[0], behind[1]))

    ahead, _, final = lax.fori_loop(
        0,
        (cycle_size - 1) // 2,
        both_turn,
        (stacked, stacked, absorb(empty, keys_read, values_read)),
    )
    ahead = forward(ahead)
    final = absorb(final, ahead[0], ahead[1])
    attended = (
        (final[2] / final[1][..., None]).astype(jnp.bfloat16).reshape(token_count, heads_here * HD)
    )
    partial_value = jnp.dot(
        attended,
        lax.all_gather(out_weight, "ctx", axis=1, tiled=True),
        preferred_element_type=jnp.float32,
    )
    summed = lax.psum_scatter(
        partial_value.astype(jnp.bfloat16), ("head", "sub"), scatter_dimension=1, tiled=True
    )
    return summed


def solution(mesh):
    return jax.shard_map(
        on_device,
        mesh=mesh,
        in_specs=(
            P(("groups", "ctx"), ("head", "sub")),
            P(("groups", "ctx"), "head"),
            P(("groups", "ctx"), "head"),
            P(("head", "sub"), "ctx"),
        ),
        out_specs=P(("groups", "ctx"), ("head", "sub")),
        check_vma=False,
    )
```

profile of v0, /device:TPU:0, one launch (start us, length us, event | category | flops | bytes accessed | tf_op | source)
XLA Modules:
  0.0 442.7 jit_solution(13286977916574830429)
XLA Ops:
  6.5 0.0 all-gather.2.cloned.1.call-start
  6.5 0.7 all-gather.2.cloned.1.call-update
  7.3 0.0 reduce-scatter.2.cloned.1.call-start
  7.3 1.2 copy.17
  8.5 1.2 copy.20
  9.8 0.2 copy.50
  10.0 0.2 copy.22
  10.2 3.1 collective-permute-start
  13.3 2.1 collective-permute-start.1
  15.4 0.0 copy-done
  15.4 0.4 copy.51
  15.8 1.5 bitcast_reduce_fusion.3
  17.4 8.0 %collective-permute-done = bf16[2,384,2,128]{3,1,2,0:T(8,128)(2,1)S(1)} collective-permute-done((bf16[2,384,2,128]{3,1,2,0:T(8,128)(2,1)S(1)}, bf16[2,384,2,128]{3,1,2,0:T(8,128)(2,1)S(1)}, u32[]{:S(2)}, u32[]{:S(2)}) %collective-permute-start) | collective-permute-done | bytes 393248 | tf_op jit(solution)/shard_map/while/body/eval_jaxpr/ppermute | solution.py:14
  25.3 0.0 collective-permute-start.2
  25.4 1.5 bitcast_reduce_fusion.2
  26.8 12.9 %collective-permute-done.1 = bf16[2,384,2,128]{3,1,2,0:T(8,128)(2,1)S(1)} collective-permute-done((bf16[2,384,2,128]{3,1,2,0:T(8,128)(2,1)S(1)}, bf16[2,384,2,128]{3,1,2,0:T(8,128)(2,1)S(1)}, u32[]{:S(2)}, u32[]{:S(2)}) %collective-permute-start.1) | collective-permute-done | bytes 393248 | tf_op jit(solution)/shard_map/while/body/eval_jaxpr/ppermute | solution.py:14
  39.7 5.1 %bitcast_reduce_fusion.1 = (f32[384,2,8]{0,2,1:T(8,128)S(1)}, f32[2,384,384,8]{2,1,3,0:T(8,128)}) fusion(bf16[384,2,8,128]{3,2,1,0:T(8,128)(2,1)S(1)} %bitcast.138, bf16[2,384,2,128]{3,1,2,0:T(8,128)(2,1)S(1)} %collective-permute-done.1), kind=kOutput, calls=%fused_computation.4 | convolution fusion | flops 608692224 | bytes 11231232 | tf_op jit(solution)/shard_map/while/body/eval_jaxpr/tngd,knd->tngk/dot_general | solution.py:38
  44.8 0.0 copy-done.1
  44.8 7.7 %collective-permute-done.2 = bf16[2,384,2,128]{3,1,2,0:T(8,128)(2,1)S(1)} collective-permute-done((bf16[2,384,2,128]{3,1,2,0:T(8,128)(2,1)S(1)}, bf16[2,384,2,128]{3,1,2,0:T(8,128)(2,1)S(1)}, u32[]{:S(2)}, u32[]{:S(2)}) %collective-permute-start.2) | collective-permute-done | bytes 393248 | tf_op jit(solution)/shard_map/ppermute | solution.py:14
  52.5 5.1 %bitcast_reduce_fusion = (f32[384,2,8]{0,2,1:T(8,128)S(1)}, f32[2,384,384,8]{2,1,3,0:T(8,128)}) fusion(bf16[384,2,8,128]{3,2,1,0:T(8,128)(2,1)S(1)} %bitcast.139, bf16[2,384,2,128]{3,1,2,0:T(8,128)(2,1)S(1)} %collective-permute-done.2), kind=kOutput, calls=%fused_computation.1 | convolution fusion | flops 608692224 | bytes 11231232 | tf_op jit(solution)/shard_map/tngd,knd->tngk/dot_general | solution.py:38
  57.6 0.0 copy-done.3
  57.6 1.6 fusion.4
  59.2 0.0 copy-done.5
  59.2 1.6 fusion.6
  60.8 5.3 %fusion.8 = f32[384,2,8]{0,2,1:T(8,128)S(1)} fusion(f32[2,384,384,8]{2,1,3,0:T(8,128)} %get-tuple-element.38, f32[384,2,8]{0,2,1:T(8,128)S(1)} %get-tuple-element.30), kind=kLoop, calls=%fused_computation.16 | loop fusion | flops 7071744 | bytes 9486336 | tf_op jit(solution)/shard_map/while/body/eval_jaxpr/reduce_sum | solution.py:44
  66.1 5.2 %fusion.10 = f32[384,2,8]{0,2,1:T(8,128)S(1)} fusion(f32[2,384,384,8]{2,1,3,0:T(8,128)} %get-tuple-element.36, f32[384,2,8]{0,2,1:T(8,128)S(1)} %get-tuple-element.28), kind=kLoop, calls=%fused_computation.18 | loop fusion | flops 7071744 | bytes 9486336 | tf_op jit(solution)/shard_map/reduce_sum | solution.py:44
  71.4 0.0 copy-start.2
  71.4 0.7 multiply_add_fusion
  72.0 2.0 fusion.18
  74.1 0.0 copy-done.2
  74.1 0.0 slice-start.2
  74.1 0.0 copy-start.4
  74.1 0.0 slice-start.3
  74.1 0.0 slice-start.4
  74.2 1.8 fusion.16
  75.9 0.1 slice-done.2
  76.0 0.1 copy-done.4
  76.1 0.0 copy-start.9
  76.1 0.0 copy-start.10
  76.1 1.7 fusion.14
  77.9 1.1 slice-done.5
  78.9 0.0 copy-done.6
  79.0 0.0 copy-done.10
  79.0 3.6 fusion.29
  82.6 296.6 %all-gather.2.cloned.1.call-done = bf16[2048,5120]{1,0:T(8,128)(2,1)} async-done(((bf16[2048,1280]{1,0:T(8,128)(2,1)}), bf16[2048,5120]{1,0:T(8,128)(2,1)}) %all-gather.2.cloned.1.call-update) | async-done | bytes 20971536 | tf_op jit(solution)/shard_map/all_gather | solution.py:83
  379.1 14.5 %convolution_convert_fusion = bf16[384,5120]{1,0:T(8,128)(2,1)} fusion(bf16[384,2048]{0,1:T(8,128)(2,1)} %bitcast.147, bf16[2048,5120]{1,0:T(8,128)(2,1)} %all-gather.2.cloned.1.call-done), kind=kOutput, calls=%fused_computation.20 | convolution fusion | flops 8055029760 | bytes 26476544 | tf_op jit(solution)/shard_map/dot_general | solution.py:81
  393.7 0.0 reduce-scatter.2.cloned.1.call-update
  393.7 42.2 %reduce-scatter.2.cloned.1.call-done = bf16[384,1280]{1,0:T(8,128)(2,1)} async-done(((bf16[384,5120]{1,0:T(8,128)(2,1)}), bf16[384,1280]{1,0:T(8,128)(2,1)}) %reduce-scatter.2.cloned.1.call-update) | async-done | bytes 983056 | tf_op jit(solution)/shard_map/reduce_scatter | solution.py:86
  (22 shorter events, 0.1 us)
Async XLA Ops:
  6.5 8.9 %copy-start = (bf16[384,2048]{1,0:T(8,128)(2,1)S(1)}, bf16[384,2048]{1,0:T(8,128)(2,1)}, u32[]{:S(2)}) copy-start(bf16[384,2048]{1,0:T(8,128)(2,1)} %param.4) | copy-start | bytes 4718596
  6.5 372.6 %all-gather.2.cloned.1.call-start = ((), (), s32[]{:S(2)}) async-start(), calls=%async_computation.1 | async-start | bytes 26214400 | tf_op jit(solution)/shard_map/all_gather | solution.py:83
  7.3 428.7 %reduce-scatter.2.cloned.1.call-start = ((), (), s32[]{:S(2)}) async-start(), calls=%async_computation.2 | async-start | bytes 4915200 | tf_op jit(solution)/shard_map/reduce_scatter | solution.py:86
  10.2 15.1 %collective-permute-start = (bf16[2,384,2,128]{3,1,2,0:T(8,128)(2,1)S(1)}, bf16[2,384,2,128]{3,1,2,0:T(8,128)(2,1)S(1)}, u32[]{:S(2)}, u32[]{:S(2)}) collective-permute-start(bf16[2,384,2,128]{3,1,2,0:T(8,128)(2,1)S(1)} %pad_maximum_fusion), channel_id=1, source_target_pairs={{12,0},{0,4},{4,8},{8,12},{13,1},{1,5},{5,9},{9,13},{14,2},{2,6},{... | collective-permute-start | bytes 1179656 | tf_op jit(solution)/shard_map/while/body/eval_jaxpr/ppermute | solution.py:14
  13.3 26.4 %collective-permute-start.1 = (bf16[2,384,2,128]{3,1,2,0:T(8,128)(2,1)S(1)}, bf16[2,384,2,128]{3,1,2,0:T(8,128)(2,1)S(1)}, u32[]{:S(2)}, u32[]{:S(2)}) collective-permute-start(bf16[2,384,2,128]{3,1,2,0:T(8,128)(2,1)S(1)} %pad_maximum_fusion), channel_id=1, source_target_pairs={{4,0},{8,4},{12,8},{0,12},{5,1},{9,5},{13,9},{1,13},{6,2},{10,6},{... | collective-permute-start | bytes 1179656 | tf_op jit(solution)/shard_map/while/body/eval_jaxpr/ppermute | solution.py:14
  25.3 19.5 %copy-start.1 = (bf16[2,384,2,128]{3,1,2,0:T(8,128)(2,1)}, bf16[2,384,2,128]{3,1,2,0:T(8,128)(2,1)S(1)}, u32[]{:S(2)}) copy-start(bf16[2,384,2,128]{3,1,2,0:T(8,128)(2,1)S(1)} %collective-permute-done) | copy-start | bytes 1179652
  25.3 27.2 %collective-permute-start.2 = (bf16[2,384,2,128]{3,1,2,0:T(8,128)(2,1)S(1)}, bf16[2,384,2,128]{3,1,2,0:T(8,128)(2,1)S(1)}, u32[]{:S(2)}, u32[]{:S(2)}) collective-permute-start(bf16[2,384,2,128]{3,1,2,0:T(8,128)(2,1)S(1)} %collective-permute-done), channel_id=1, source_target_pairs={{12,0},{0,4},{4,8},{8,12},{13,1},{1,5},{5,9},{9,13},{14,2},{2,6},{... | collective-permute-start | bytes 1179656 | tf_op jit(solution)/shard_map/ppermute | solution.py:14
  39.7 17.9 %copy-start.3 = (bf16[2,384,2,128]{3,1,2,0:T(8,128)(2,1)}, bf16[2,384,2,128]{3,1,2,0:T(8,128)(2,1)S(1)}, u32[]{:S(2)}) copy-start(bf16[2,384,2,128]{3,1,2,0:T(8,128)(2,1)S(1)} %collective-permute-done.1) | copy-start | bytes 1179652
  52.5 6.7 %copy-start.5 = (bf16[2,384,2,128]{3,1,2,0:T(8,128)(2,1)}, bf16[2,384,2,128]{3,1,2,0:T(8,128)(2,1)S(1)}, u32[]{:S(2)}) copy-start(bf16[2,384,2,128]{3,1,2,0:T(8,128)(2,1)S(1)} %collective-permute-done.2) | copy-start | bytes 1179652
  71.4 2.7 copy-start.2
  72.0 3.9 slice-start
  72.0 3.9 slice-start.1
  74.1 1.9 slice-start.2
  74.1 2.0 copy-start.4
  74.1 3.7 slice-start.3
  74.1 3.7 slice-start.4
  76.1 2.9 slice-start.5
  76.1 2.9 copy-start.6
  76.1 2.9 copy-start.7
  76.1 2.9 copy-start.8
  76.1 2.9 copy-start.9
  76.1 2.9 copy-start.10
Sparse Core Ops, SparseCore 0:
  8.9 370.1 all-gather.1
  393.8 42.0 reduce-scatter.1
where the time goes:
time: 443 us
  waiting for transfers between devices  368 us (83%)
  matrix products  36.8 us (8%)
  other arithmetic  14.5 us (3%)
  between operations  13.7 us (3%)
  starting transfers between devices  5.24 us (1%)
  local copies, waits for them, and re-layouts  4.47 us (1%)
    all_gather x1, waiting for transfers between devices, on_device(): lax.all_gather(out_weight, 'ctx', axis=1, tiled=True)  297 us
    reduce_scatter x1, waiting for transfers between devices, on_device(): lax.psum_scatter(partial_value.astype(jnp.bfloat16), ('head', 'sub'), sca...  42.2 us
    ppermute x3, waiting for transfers between devices, from_behind(): return lax.ppermute(block, axis, route)  28.6 us
    dot_general x1, matrix products, on_device(): jnp.dot(attended, lax.all_gather(out_weight, 'ctx', axis=1, tiled=True),...  14.5 us
    reduce_sum x4, other arithmetic, absorb(): new_sum = old_sum * shrink + jnp.sum(expo, axis=-1)  13.7 us
    dot_general x4, matrix products, absorb(): jnp.einsum('tngd,knd->tngk', grouped, key_block, preferred_element_type=j...  13.2 us
    dot_general x4, matrix products, absorb(): jnp.einsum('tngk,knd->tngd', expo.astype(jnp.bfloat16), value_block, pref...  9.13 us
  transfers between devices with their start and end apart: 5, of which 5 were waited for; matrix products, arithmetic and copies ran while one was open for 9% of the time, Pallas kernels for 0%

commit v1 on v0

--- a/solution.py
+++ b/solution.py
@@ -6,6 +6,14 @@
 QH = 64
 KVH = 8
 HD = 128
+
+
+def islands_deliver(arr_in, axis_k):
+    arr_in = jnp.moveaxis(arr_in, 0, axis_k)
+    arr_out = arr_in.shape
+    return arr_in.reshape(
+        *arr_out[:axis_k], arr_out[axis_k] * arr_out[axis_k + 1], *arr_out[axis_k + 2 :]
+    )
 
 
 def from_behind(block, axis, distance):
@@ -78,10 +86,24 @@
     attended = (
         (final[2] / final[1][..., None]).astype(jnp.bfloat16).reshape(token_count, heads_here * HD)
     )
+
+    def joints_carry(v0, net_axis, axis_no=1):
+        k_all = lax.psum(1, net_axis)
+        leaves = [(w, (w + 1) % k_all) for w in range(k_all)]
+        chunks = [(i0, dev) for dev, i0 in leaves]
+        near, outer = ([], [])
+        for to_i in tuple(range(k_all - 1)):
+            if to_i % 2 == 0:
+                near.append(lax.ppermute(near[-1] if near else v0, net_axis, leaves))
+            else:
+                outer.append(lax.ppermute(outer[-1] if outer else v0, net_axis, chunks))
+        work_now = jnp.stack([*near[::-1], v0, *outer], 0)
+        mat_out = lax.axis_index(net_axis) - len(near)
+        work_now = work_now[(jnp.arange(k_all) - mat_out) % k_all]
+        return islands_deliver(work_now, axis_no)
+
     partial_value = jnp.dot(
-        attended,
-        lax.all_gather(out_weight, "ctx", axis=1, tiled=True),
-        preferred_element_type=jnp.float32,
+        attended, joints_carry(out_weight, "ctx"), preferred_element_type=jnp.float32
     )
     summed = lax.psum_scatter(
         partial_value.astype(jnp.bfloat16), ("head", "sub"), scatter_dimension=1, tiled=True

time: 443 us -> 531 us (1.20)
  local copies, waits for them, and re-layouts: 4.47 us -> 58.8 us
  other arithmetic: 14.5 us -> 43.5 us
  waiting for transfers between devices: 368 us -> 356 us
  matrix products: 36.8 us -> 48.1 us
    all_gather x1 -> x0, waiting for transfers between devices: 297 us -> none  [on_device(): lax.all_gather(out_weight, 'ctx', axis=1, tiled=True)]
    ppermute x3, waiting for transfers between devices: 28.6 us -> 234 us  [from_behind(): return lax.ppermute(block, axis, route)]
    ppermute x0 -> x3, waiting for transfers between devices: none -> 79.9 us  [the longest x2 79.9 us: joints_carry(): near.append(lax.ppermute(near[-1] if near else v0, net_axis, leaves))]
    transpose x0 -> x1, local copies, waits for them, and re-layouts: none -> 27.3 us  [islands_deliver(): arr_in = jnp.moveaxis(arr_in, 0, axis_k)]
    gather x0 -> x4, local copies, waits for them, and re-layouts: none -> 26.9 us  [joints_carry(): work_now = work_now[(jnp.arange(k_all) - mat_out) % k_all]]
    transpose x0 -> x1, other arithmetic: none -> 17.3 us  [islands_deliver(): arr_in = jnp.moveaxis(arr_in, 0, axis_k)]
    dot_general x4, matrix products: 9.13 us -> 21 us  [absorb(): jnp.einsum('tngk,knd->tngd', expo.astype(jnp.bfloat16), value_block, pref...]
    another operation x0 -> x1, other arithmetic: none -> 8.02 us  [joints_carry(): work_now = jnp.stack([*near[::-1], v0, *outer], 0)]
  transfers between devices with their start and end apart: 5 -> 7, of which waited for: 5 -> 4; matrix products, arithmetic and copies ran while one was open for 9% -> 10% of each run, Pallas kernels for 0% -> 0%
where the time goes in v1:
time: 531 us; the launch traced here: 529 us
  waiting for transfers between devices  356 us (67%)
  local copies, waits for them, and re-layouts  58.8 us (11%)
  matrix products  48.1 us (9%)
  other arithmetic  43.5 us (8%)
  between operations  13.6 us (3%)
  starting transfers between devices  9.2 us (2%)
    ppermute x3, waiting for transfers between devices, from_behind(): return lax.ppermute(block, axis, route)  234 us
    ppermute x2, waiting for transfers between devices, joints_carry(): near.append(lax.ppermute(near[-1] if near else v0, net_axis, leaves))  79.9 us
    reduce_scatter x1, waiting for transfers between devices, on_device(): lax.psum_scatter(partial_value.astype(jnp.bfloat16), ('head', 'sub'), sca...  41.7 us
    transpose x1, local copies, waits for them, and re-layouts, islands_deliver(): arr_in = jnp.moveaxis(arr_in, 0, axis_k)  27.3 us
    gather x4, local copies, waits for them, and re-layouts, joints_carry(): work_now = work_now[(jnp.arange(k_all) - mat_out) % k_all]  26.9 us
    dot_general x4, matrix products, absorb(): jnp.einsum('tngk,knd->tngd', expo.astype(jnp.bfloat16), value_block, pref...  21 us
    transpose x1, other arithmetic, islands_deliver(): arr_in = jnp.moveaxis(arr_in, 0, axis_k)  17.3 us
    dot_general x1, matrix products, on_device(): jnp.dot(attended, joints_carry(out_weight, 'ctx'), preferred_element_type...  13.9 us
  transfers between devices with their start and end apart: 7, of which 4 were waited for; matrix products, arithmetic and copies ran while one was open for 10% of the time, Pallas kernels for 0%

profile of v1, /device:TPU:0, one launch (start us, length us, event | category | flops | bytes accessed | tf_op | source)
XLA Modules:
  0.0 529.1 jit_solution(13869403447212529623)
XLA Ops:
  6.5 0.0 reduce-scatter.2.cloned.1.call-start
  6.5 3.1 collective-permute-start.3
  9.6 1.2 copy.35
  10.8 1.2 copy.32
  12.1 0.2 copy.37
  12.3 0.2 copy.66
  12.5 2.1 collective-permute-start.1
  14.6 0.0 collective-permute-start
  14.6 3.8 collective-permute-start.5
  18.4 1.8 copy.67
  20.2 1.5 bitcast_reduce_fusion.3
  21.8 120.9 %collective-permute-done = bf16[2,384,2,128]{3,1,2,0:T(8,128)(2,1)S(1)} collective-permute-done((bf16[2,384,2,128]{3,1,2,0:T(8,128)(2,1)S(1)}, bf16[2,384,2,128]{3,1,2,0:T(8,128)(2,1)S(1)}, u32[]{:S(2)}, u32[]{:S(2)}) %collective-permute-start) | collective-permute-done | bytes 393248 | tf_op jit(solution)/shard_map/while/body/eval_jaxpr/ppermute | solution.py:22
  142.7 0.0 collective-permute-start.2
  142.7 1.5 bitcast_reduce_fusion.2
  144.1 0.0 collective-permute-done.1
  144.1 5.1 bitcast_reduce_fusion.1
  149.3 113.3 %collective-permute-done.2 = bf16[2,384,2,128]{3,1,2,0:T(8,128)(2,1)S(1)} collective-permute-done((bf16[2,384,2,128]{3,1,2,0:T(8,128)(2,1)S(1)}, bf16[2,384,2,128]{3,1,2,0:T(8,128)(2,1)S(1)}, u32[]{:S(2)}, u32[]{:S(2)}) %collective-permute-start.2) | collective-permute-done | bytes 393248 | tf_op jit(solution)/shard_map/ppermute | solution.py:22
  262.6 5.1 bitcast_reduce_fusion
  267.7 0.0 collective-permute-done.3
  267.7 0.2 collective-permute-start.4
  267.9 5.2 fusion.10
  273.2 5.3 fusion.8
  278.5 1.6 fusion.6
  280.0 1.6 fusion.4
  281.7 3.5 fusion.18
  285.2 5.4 %fusion.14 = f32[2,128,384,8]{2,1,3,0:T(8,128)S(1)} fusion(f32[2,384,384,8]{2,1,3,0:T(8,128)} %get-tuple-element.40, f32[384,2,8]{0,2,1:T(8,128)S(1)} %get-tuple-element.30, bf16[2,384,2,128]{3,1,2,0:T(8,128)(2,1)S(1)} %collective-permute-done.1), kind=kOutput, calls=%fused_computation.28 | convolution fusion | flops 611057664 | bytes 12804096 | tf_op jit(solution)/shard_map/while/body/eval_jaxpr/tngk,knd->tngd/dot_general | solution.py:53
  290.6 0.0 copy-start
  290.6 0.0 slice-start
  290.7 3.4 fusion.16
  294.0 0.0 copy-done
  294.0 0.0 slice-start.1
  294.0 8.7 %fusion.29 = bf16[384,2,8,128]{0,3,2,1:T(8,128)(2,1)} fusion(f32[2,128,384,8]{2,1,3,0:T(8,128)S(1)} %fusion.14, f32[2,128,384,8]{2,1,3,0:T(8,128)} %fusion.16, f32[2,128,384,8]{2,1,3,0:T(8,128)S(1)} %copy-done, f32[2,384,384,8]{2,1,3,0:T(8,128)} %get-tuple-element.38, f32[384,2,8]{0,2,1:T(8,128)S(1)} %get-tuple-element.28, ...), kind=kOutput, calls=%fused_computation.41 | convolution fusion | flops 618135552 | bytes 20791296 | tf_op jit(solution)/shard_map/tngk,knd->tngd/dot_general | solution.py:53
  302.7 0.0 collective-permute-done.5
  302.7 79.9 %collective-permute-done.4 = bf16[2048,1280]{1,0:T(8,128)(2,1)S(1)} collective-permute-done((bf16[2048,1280]{1,0:T(8,128)(2,1)}, bf16[2048,1280]{1,0:T(8,128)(2,1)S(1)}, u32[]{:S(2)}, u32[]{:S(2)}) %collective-permute-start.4) | collective-permute-done | bytes 5242912 | tf_op jit(solution)/shard_map/ppermute | solution.py:97
  382.7 0.0 slice-done
  382.7 0.0 slice-done.1
  382.7 4.4 pad_maximum_fusion.1
  387.1 8.0 %pad_maximum_fusion = bf16[4,2048,1280]{2,1,0:T(8,128)(2,1)S(1)} fusion(bf16[1,2048,1280]{2,1,0:T(8,128)(2,1)} %bitcast.35, bf16[1,2048,1280]{2,1,0:T(8,128)(2,1)S(1)} %bitcast.151, bf16[1,2048,1280]{2,1,0:T(8,128)(2,1)} %bitcast.33, bf16[1,2048,1280]{2,1,0:T(8,128)(2,1)S(1)} %bitcast.153), kind=kLoop, calls=%fused_computation.3 | loop fusion | flops 31457280 | bytes 41943040 | tf_op jit(solution)/shard_map/stack | solution.py:100
  395.1 5.8 %fusion.54 = (bf16[4,768,1280]{2,1,0:T(8,128)(2,1)}, bf16[4,768,1280]{2,1,0:T(8,128)(2,1)}) fusion(bf16[4,2048,1280]{2,1,0:T(8,128)(2,1)S(1)} %pad_maximum_fusion), kind=kLoop, calls=%fused_computation.86 | loop fusion | bytes 31457280 | tf_op jit(solution)/shard_map/gather | solution.py:102
  400.9 5.6 %gather_fusion.2 = bf16[4,512,1280]{2,1,0:T(8,128)(2,1)} fusion(bf16[4,512,1280]{2,1,0:T(8,128)(2,1)} %pad_maximum_fusion.1, s32[1024]{0:T(1024)S(1)} %pad_clamp_fusion), kind=kCustom, calls=%fused_computation.2 | custom fusion | bytes 10485776 | tf_op jit(solution)/shard_map/gather | solution.py:102
  406.5 7.7 %gather_fusion.1 = bf16[4,768,1280]{2,1,0:T(8,128)(2,1)} fusion(bf16[4,768,1280]{2,1,0:T(8,128)(2,1)} %get-tuple-element.34, s32[1024]{0:T(1024)S(1)} %pad_clamp_fusion), kind=kCustom, calls=%fused_computation.1 | custom fusion | bytes 15728656 | tf_op jit(solution)/shard_map/gather | solution.py:102
  414.2 7.7 %gather_fusion = bf16[4,768,1280]{2,1,0:T(8,128)(2,1)} fusion(bf16[4,768,1280]{2,1,0:T(8,128)(2,1)} %get-tuple-element.33, s32[1024]{0:T(1024)S(1)} %pad_clamp_fusion), kind=kCustom, calls=%fused_computation | custom fusion | bytes 15728656 | tf_op jit(solution)/shard_map/gather | solution.py:102
  422.0 17.3 %maximum_bitcast_fusion = bf16[2048,4,1280]{2,0,1:T(8,128)(2,1)} fusion(bf16[4,512,1280]{2,1,0:T(8,128)(2,1)} %gather_fusion.2, bf16[4,768,1280]{2,1,0:T(8,128)(2,1)} %gather_fusion.1, bf16[4,768,1280]{2,1,0:T(8,128)(2,1)} %gather_fusion), kind=kLoop, calls=%fused_computation.4 | loop fusion | flops 62914560 | bytes 41943040 | tf_op jit(solution)/shard_map/transpose | solution.py:12
  439.3 27.3 %copy.47 = bf16[2048,4,1280]{0,2,1:T(8,128)(2,1)} copy(bf16[2048,4,1280]{2,0,1:T(8,128)(2,1)} %maximum_bitcast_fusion) | data formatting | bytes 41943040 | tf_op jit(solution)/shard_map/transpose | solution.py:12
  466.6 0.0 copy-done.1
  466.6 13.9 %convolution_convert_fusion = bf16[384,5120]{1,0:T(8,128)(2,1)} fusion(bf16[384,2048]{0,1:T(8,128)(2,1)S(1)} %bitcast.159, bf16[2048,5120]{0,1:T(8,128)(2,1)} %bitcast.147), kind=kOutput, calls=%fused_computation.25 | convolution fusion | flops 8055029760 | bytes 26476544 | tf_op jit(solution)/shard_map/dot_general | solution.py:105
  480.4 0.0 reduce-scatter.2.cloned.1.call-update
  480.5 41.7 %reduce-scatter.2.cloned.1.call-done = bf16[384,1280]{1,0:T(8,128)(2,1)} async-done(((bf16[384,5120]{1,0:T(8,128)(2,1)}), bf16[384,1280]{1,0:T(8,128)(2,1)}) %reduce-scatter.2.cloned.1.call-update) | async-done | bytes 983056 | tf_op jit(solution)/shard_map/reduce_scatter | solution.py:108
  (8 shorter events, 0.2 us)
Async XLA Ops:
  6.5 515.7 %reduce-scatter.2.cloned.1.call-start = ((), (), s32[]{:S(2)}) async-start(), calls=%async_computation.1 | async-start | bytes 4915200 | tf_op jit(solution)/shard_map/reduce_scatter | solution.py:108
  6.5 261.2 %collective-permute-start.3 = (bf16[2048,1280]{1,0:T(8,128)(2,1)}, bf16[2048,1280]{1,0:T(8,128)(2,1)}, u32[]{:S(2)}, u32[]{:S(2)}) collective-permute-start(bf16[2048,1280]{1,0:T(8,128)(2,1)} %param.7), channel_id=1, source_target_pairs={{0,4},{4,8},{8,12},{12,0},{1,5},{5,9},{9,13},{13,1},{2,6},{6,10},{... | collective-permute-start | bytes 15728648 | tf_op jit(solution)/shard_map/ppermute | solution.py:97
  12.5 131.6 %collective-permute-start.1 = (bf16[2,384,2,128]{3,1,2,0:T(8,128)(2,1)S(1)}, bf16[2,384,2,128]{3,1,2,0:T(8,128)(2,1)S(1)}, u32[]{:S(2)}, u32[]{:S(2)}) collective-permute-start(bf16[2,384,2,128]{3,1,2,0:T(8,128)(2,1)S(1)} %pad_maximum_fusion.2), channel_id=1, source_target_pairs={{4,0},{8,4},{12,8},{0,12},{5,1},{9,5},{13,9},{1,13},{6,2},{10,6},{... | collective-permute-start | bytes 1179656 | tf_op jit(solution)/shard_map/while/body/eval_jaxpr/ppermute | solution.py:22
  14.6 128.1 %collective-permute-start = (bf16[2,384,2,128]{3,1,2,0:T(8,128)(2,1)S(1)}, bf16[2,384,2,128]{3,1,2,0:T(8,128)(2,1)S(1)}, u32[]{:S(2)}, u32[]{:S(2)}) collective-permute-start(bf16[2,384,2,128]{3,1,2,0:T(8,128)(2,1)S(1)} %pad_maximum_fusion.2), channel_id=1, source_target_pairs={{12,0},{0,4},{4,8},{8,12},{13,1},{1,5},{5,9},{9,13},{14,2},{2,6},{... | collective-permute-start | bytes 1179656 | tf_op jit(solution)/shard_map/while/body/eval_jaxpr/ppermute | solution.py:22
  14.6 288.1 %collective-permute-start.5 = (bf16[2048,1280]{1,0:T(8,128)(2,1)}, bf16[2048,1280]{1,0:T(8,128)(2,1)}, u32[]{:S(2)}, u32[]{:S(2)}) collective-permute-start(bf16[2048,1280]{1,0:T(8,128)(2,1)} %param.7), channel_id=1, source_target_pairs={{4,0},{8,4},{12,8},{0,12},{5,1},{9,5},{13,9},{1,13},{6,2},{10,6},{... | collective-permute-start | bytes 15728648 | tf_op jit(solution)/shard_map/ppermute | solution.py:99
  142.7 119.9 %collective-permute-start.2 = (bf16[2,384,2,128]{3,1,2,0:T(8,128)(2,1)S(1)}, bf16[2,384,2,128]{3,1,2,0:T(8,128)(2,1)S(1)}, u32[]{:S(2)}, u32[]{:S(2)}) collective-permute-start(bf16[2,384,2,128]{3,1,2,0:T(8,128)(2,1)S(1)} %collective-permute-done), channel_id=1, source_target_pairs={{12,0},{0,4},{4,8},{8,12},{13,1},{1,5},{5,9},{9,13},{14,2},{2,6},{... | collective-permute-start | bytes 1179656 | tf_op jit(solution)/shard_map/ppermute | solution.py:22
  267.7 115.0 %collective-permute-start.4 = (bf16[2048,1280]{1,0:T(8,128)(2,1)}, bf16[2048,1280]{1,0:T(8,128)(2,1)S(1)}, u32[]{:S(2)}, u32[]{:S(2)}) collective-permute-start(bf16[2048,1280]{1,0:T(8,128)(2,1)} %collective-permute-done.3), channel_id=1, source_target_pairs={{0,4},{4,8},{8,12},{12,0},{1,5},{5,9},{9,13},{13,1},{2,6},{6,10},{... | collective-permute-start | bytes 15728648 | tf_op jit(solution)/shard_map/ppermute | solution.py:97
  290.6 3.4 copy-start
  290.6 92.0 %slice-start = ((s8[5242880]{0:T(1024)(128)(4,1)}), s8[1048576]{0:T(1024)(128)(4,1)S(1)}, s32[]{:S(2)}) async-start(s8[5242880]{0:T(1024)(128)(4,1)} %bitcast.148), calls=%async_computation.2 | async-start | bytes 2097152
  294.0 88.6 %slice-start.1 = ((s8[5242880]{0:T(1024)(128)(4,1)}), s8[4194304]{0:T(1024)(128)(4,1)S(1)}, s32[]{:S(2)}) async-start(s8[5242880]{0:T(1024)(128)(4,1)} %bitcast.148), calls=%async_computation.3 | async-start | bytes 8388608
  439.3 27.3 %copy-start.1 = (bf16[384,2,8,128]{0,3,2,1:T(8,128)(2,1)S(1)}, bf16[384,2,8,128]{0,3,2,1:T(8,128)(2,1)}, u32[]{:S(2)}) copy-start(bf16[384,2,8,128]{0,3,2,1:T(8,128)(2,1)} %fusion.29) | copy-start | bytes 4718596
Sparse Core Ops, SparseCore 0:
  480.6 41.5 reduce-scatter.1
